TPU v7x, 512 devices: a whole 4x4x16 slice. The times are simulated.
512 devices in a mesh: row: 16 (over y, x), col: 32 (over z, core).
Axes of the slice: x: 4, y: 4, z: 16, core: 2. Of those that a mesh axis runs over, the one named last changes fastest.
Arguments:
- panel: bfloat16 [4, 16, 512, 512], P(None, 'row', 'col'), may hold values from -1.1953125 to 1.1953125
- inverse_factor: bfloat16 [512, 512], replicated
- slot_rows: int32 [16, 32, 2], P('row', 'col'), may hold values from 0 to 63, as said below
- slot_cols: int32 [16, 32, 2], P('row', 'col'), may hold values from 0 to 63, as said below
- live_count: int32 [16, 32], P('row', 'col'), may hold values from 0 to 2
Outputs:
- contrib: bfloat16 [16, 32, 2, 512, 512], P('row', 'col')
Inputs may be any that keep to these rules, and one draw needn't show every extreme that they name: slot_rows[r, c, s] is congruent to r modulo 16; for s < live_count[r, c] the slots of one position name distinct blocks with slot_rows >= slot_cols; the other slots are ignored. slot_cols[r, c, s] is congruent to c modulo 32.
All inputs are finite; a program needn't handle non-finite values.
Results may differ from a plain program's by a relative error of at most 0.0054.
Values may be sent and summed in bfloat16 or wider, within the bound.
No kernel may reach another device: no remote copies, remote signals or barrier semaphores. Data moves between devices by JAX's collectives and lax.ppermute only.
A program may use at most 64 MiB of HBM per device.

v0:
```python
import jax
import jax.numpy as jnp
from jax import lax
from jax.sharding import PartitionSpec as P


def broadcast(value, axis, source):
    kept = jnp.where(lax.axis_index(axis) == source, value, 0).astype(value.dtype)
    return lax.psum(kept, axis)


def body(panel, inverse_factor, slot_rows, slot_cols, live_count):
    panel_count, _, part_rows, tile_width = panel.shape
    grid_rows = lax.axis_size("row")
    grid_cols = lax.axis_size("col")
    col_ratio = grid_cols // grid_rows
    column_count = panel_count // col_ratio
    solved = jnp.dot(
        panel.reshape(-1, tile_width), inverse_factor, preferred_element_type=jnp.float32
    )
    solved = solved.astype(jnp.bfloat16).reshape(panel_count, 1, part_rows, tile_width)
    row_blocks = lax.all_gather(solved, "col", axis=2, tiled=True).reshape(
        panel_count, tile_width, tile_width
    )
    position = lax.axis_index("col")
    grouped = row_blocks.reshape(column_count, col_ratio, tile_width, tile_width)
    picked = lax.dynamic_index_in_dim(grouped, position // grid_rows, 1, keepdims=False)
    col_blocks = broadcast(picked, "row", position % grid_rows)
    slot_total = slot_rows.shape[-1]
    rows_here = slot_rows.reshape(-1)
    cols_here = slot_cols.reshape(-1)
    live_here = live_count.reshape(())
    result = jnp.zeros((slot_total, tile_width, tile_width), jnp.bfloat16)

    def update(slot, current):
        left_tile = lax.dynamic_index_in_dim(
            row_blocks, rows_here[slot] // grid_rows, 0, keepdims=False
        )
        right_tile = lax.dynamic_index_in_dim(
            col_blocks, cols_here[slot] // grid_cols, 0, keepdims=False
        )
        product = lax.dot_general(
            left_tile, right_tile, (((1,), (1,)), ((), ())), preferred_element_type=jnp.float32
        )
        return lax.dynamic_update_index_in_dim(current, (-product).astype(jnp.bfloat16), slot, 0)

    result = lax.fori_loop(0, live_here, update, result)
    return result.reshape(1, 1, slot_total, tile_width, tile_width)


def solution(mesh):
    placed = (
        P(None, "row", "col", None),
        P(),
        P("row", "col", None),
        P("row", "col", None),
        P("row", "col"),
    )
    return jax.shard_map(
        body,
        mesh=mesh,
        in_specs=placed,
        out_specs=P("row", "col", None, None, None),
        check_vma=False,
    )
```

profile of v0, /device:TPU:32, one launch (start us, length us, event | category | flops | bytes accessed | tf_op | source)
XLA Modules:
  0.0 229.6 jit_solution(7024908279362446910)
XLA Ops:
  6.5 0.0 copy-start
  6.5 0.0 all-gather.2.cloned.1.call-start
  6.5 1.0 copy-done
  7.6 1.7 convolution_convert_fusion
  9.3 0.0 all-gather.2.cloned.1.call-update
  9.3 0.0 all-reduce.2.cloned.1.call-start
  9.4 76.0 %all-gather.2.cloned.1.call-done = bf16[4,1,512,512]{3,2,0,1:T(8,128)(2,1)} async-done(((bf16[4,1,16,512]{3,2,0,1:T(8,128)(2,1)}), bf16[4,1,512,512]{3,2,0,1:T(8,128)(2,1)}) %all-gather.2.cloned.1.call-update) | async-done | bytes 2097168 | tf_op jit(solution)/shard_map/all_gather | solution.py:22
  85.3 0.0 copy-start.2
  85.3 0.0 copy-start.3
  85.3 2.3 select_bitcast_fusion
  87.6 0.0 all-reduce.2.cloned.1.call-update
  87.7 115.9 %all-reduce.2.cloned.1.call-done = bf16[2,512,512]{2,1,0:T(8,128)(2,1)} async-done(((bf16[2,512,512]{2,1,0:T(8,128)(2,1)}), bf16[2,512,512]{2,1,0:T(8,128)(2,1)}) %all-reduce.2.cloned.1.call-update) | async-done | bytes 1048592 | tf_op jit(solution)/shard_map/psum | solution.py:9
  203.6 0.1 broadcast_in_dim.15
  203.6 0.0 copy-done.2
  203.6 0.0 copy-done.3
  203.7 18.1 %while.13 = (s32[]{:T(128)}, bf16[2,512,512]{2,1,0:T(8,128)(2,1)S(1)}, s32[]{:T(128)}, s32[2]{0:T(128)S(1)}, bf16[4,512,512]{2,1,0:T(8,128)(2,1)}, /*index=5*/s3...) while((s32[]{:T(128)}, ...), condition=%wide.region_2.3_spmd, body=%wide.region_1.2_spmd.sunk | while | flops 268959776 | bytes 1573451 | solution.py:47
  204.3 0.6 dynamic_slice.51
  207.5 0.6 dynamic_slice.50
  210.7 1.7 fusion.15
  213.1 0.6 dynamic_slice.51
  216.3 0.6 dynamic_slice.50
  219.5 1.7 fusion.15
  221.8 0.0 copy-start.1
  221.8 1.0 copy-done.1
Async XLA Ops:
  6.5 1.0 copy-start
  6.5 78.8 %all-gather.2.cloned.1.call-start = ((), (), s32[]{:S(2)}) async-start(), calls=%async_computation | async-start | bytes 2162688 | tf_op jit(solution)/shard_map/all_gather | solution.py:22
  9.3 194.3 %all-reduce.2.cloned.1.call-start = ((), (), s32[]{:S(2)}) async-start(), calls=%async_computation.1 | async-start | bytes 2097152 | tf_op jit(solution)/shard_map/psum | solution.py:9
  85.3 118.3 %copy-start.2 = (s32[1,1,2]{2,1,0:T(1,128)S(1)}, s32[1,1,2]{2,1,0:T(1,128)}, u32[]{:S(2)}) copy-start(s32[1,1,2]{2,1,0:T(1,128)} %param.9) | copy-start | bytes 28
  85.3 118.3 %copy-start.3 = (s32[1,1,2]{2,1,0:T(1,128)S(1)}, s32[1,1,2]{2,1,0:T(1,128)}, u32[]{:S(2)}) copy-start(s32[1,1,2]{2,1,0:T(1,128)} %param.10) | copy-start | bytes 28
  221.8 1.0 copy-start.1
Sparse Core Ops, SparseCore 0:
  9.5 75.7 all-gather.1
  88.6 114.9 all-reduce.1
where the time goes:
time: 230 us
  waiting for transfers between devices  192 us (83%)
  between operations  13.5 us (6%)
  loops' own time  12.4 us (5%)
  matrix products  5.03 us (2%)
  local copies, waits for them, and re-layouts  4.43 us (2%)
    psum x1, waiting for transfers between devices, broadcast(): return lax.psum(kept, axis)  116 us
    all_gather x1, waiting for transfers between devices, body(): lax.all_gather(solved, 'col', axis=2, tiled=True)  76 us
    another operation x1, loops' own time, body(): result = lax.fori_loop(0, live_here, update, result)  12.4 us
  transfers between devices with their start and end apart: 2, of which 2 were waited for; matrix products, arithmetic and copies ran while one was open for 0% of the time, Pallas kernels for 0%

commit v1 on v0

--- a/solution.py
+++ b/solution.py
@@ -2,6 +2,13 @@
 import jax.numpy as jnp
 from jax import lax
 from jax.sharding import PartitionSpec as P
+
+
+def advance_racks_in(inputs):
+    arr_now = jax.lax.axis_size("col")
+    big = jnp.concatenate([inputs] * arr_now, 2)
+    fresh = jax.lax.all_to_all(big, "col", split_axis=2, concat_axis=2, tiled=True)
+    return fresh
 
 
 def broadcast(value, axis, source):
@@ -19,9 +26,7 @@
         panel.reshape(-1, tile_width), inverse_factor, preferred_element_type=jnp.float32
     )
     solved = solved.astype(jnp.bfloat16).reshape(panel_count, 1, part_rows, tile_width)
-    row_blocks = lax.all_gather(solved, "col", axis=2, tiled=True).reshape(
-        panel_count, tile_width, tile_width
-    )
+    row_blocks = advance_racks_in(solved).reshape(panel_count, tile_width, tile_width)
     position = lax.axis_index("col")
     grouped = row_blocks.reshape(column_count, col_ratio, tile_width, tile_width)
     picked = lax.dynamic_index_in_dim(grouped, position // grid_rows, 1, keepdims=False)

time: 230 us -> 284 us (1.23)
  local copies, waits for them, and re-layouts: 4.43 us -> 28.1 us
  waiting for transfers between devices: 192 us -> 209 us
  starting transfers between devices: 0.04 us -> 15.4 us
    all_to_all x0 -> x1, waiting for transfers between devices: none -> 100 us  [advance_racks_in(): jax.lax.all_to_all(big, 'col', split_axis=2, concat_axis=2, tiled=True)]
    all_gather x1 -> x0, waiting for transfers between devices: 76 us -> none  [body(): lax.all_gather(solved, 'col', axis=2, tiled=True)]
    unnamed x8 -> x39, local copies, waits for them, and re-layouts: 2.01 us -> 22.8 us
    all_to_all x0 -> x1, starting transfers between devices: none -> 15.4 us  [advance_racks_in(): jax.lax.all_to_all(big, 'col', split_axis=2, concat_axis=2, tiled=True)]
    psum x1, waiting for transfers between devices: 116 us -> 109 us  [broadcast(): return lax.psum(kept, axis)]
  transfers between devices with their start and end apart: 2 -> 2, of which waited for: 2 -> 2; matrix products, arithmetic and copies ran while one was open for 0% -> 1% of each run, Pallas kernels for 0% -> 0%
where the time goes in v1:
time: 284 us
  waiting for transfers between devices  209 us (74%)
  local copies, waits for them, and re-layouts  28.1 us (10%)
  starting transfers between devices  15.4 us (5%)
  between operations  13.5 us (5%)
  loops' own time  12.4 us (4%)
  matrix products  4.39 us (2%)
    psum x1, waiting for transfers between devices, broadcast(): return lax.psum(kept, axis)  109 us
    all_to_all x1, waiting for transfers between devices, advance_racks_in(): jax.lax.all_to_all(big, 'col', split_axis=2, concat_axis=2, tiled=True)  100 us
    unnamed x39, local copies, waits for them, and re-layouts  22.8 us
    all_to_all x1, starting transfers between devices, advance_racks_in(): jax.lax.all_to_all(big, 'col', split_axis=2, concat_axis=2, tiled=True)  15.4 us
    another operation x1, loops' own time, body(): result = lax.fori_loop(0, live_here, update, result)  12.4 us
  transfers between devices with their start and end apart: 2, of which 2 were waited for; matrix products, arithmetic and copies ran while one was open for 1% of the time, Pallas kernels for 0%

profile of v1, /device:TPU:32, one launch (start us, length us, event | category | flops | bytes accessed | tf_op | source)
XLA Modules:
  0.0 283.5 jit_solution(7660368817296090748)
XLA Ops:
  6.5 1.0 copy-done
  7.6 1.0 convolution_convert_fusion
  8.6 0.7 constant_dynamic-update-slice_fusion.31
  9.3 0.7 constant_dynamic-update-slice_fusion.30
  10.0 0.7 constant_dynamic-update-slice_fusion.29
  10.6 0.7 constant_dynamic-update-slice_fusion.28
  11.3 0.7 constant_dynamic-update-slice_fusion.27
  12.0 0.7 constant_dynamic-update-slice_fusion.26
  12.7 0.7 constant_dynamic-update-slice_fusion.25
  13.3 0.7 constant_dynamic-update-slice_fusion.24
  14.0 0.7 constant_dynamic-update-slice_fusion.23
  14.7 0.7 constant_dynamic-update-slice_fusion.22
  15.3 0.7 constant_dynamic-update-slice_fusion.21
  16.0 0.7 constant_dynamic-update-slice_fusion.20
  16.7 0.7 constant_dynamic-update-slice_fusion.19
  17.4 0.7 constant_dynamic-update-slice_fusion.18
  18.0 0.7 constant_dynamic-update-slice_fusion.17
  18.7 0.7 constant_dynamic-update-slice_fusion.16
  19.4 0.7 constant_dynamic-update-slice_fusion.15
  20.1 0.7 constant_dynamic-update-slice_fusion.14
  20.7 0.7 constant_dynamic-update-slice_fusion.13
  21.4 0.7 constant_dynamic-update-slice_fusion.12
  22.1 0.7 constant_dynamic-update-slice_fusion.11
  22.7 0.7 constant_dynamic-update-slice_fusion.10
  23.4 0.7 constant_dynamic-update-slice_fusion.9
  24.1 0.7 constant_dynamic-update-slice_fusion.8
  24.7 0.7 constant_dynamic-update-slice_fusion.7
  25.4 0.7 constant_dynamic-update-slice_fusion.6
  26.1 0.7 constant_dynamic-update-slice_fusion.5
  26.8 0.7 constant_dynamic-update-slice_fusion.4
  27.4 0.7 constant_dynamic-update-slice_fusion.3
  28.1 0.7 constant_dynamic-update-slice_fusion.2
  28.8 0.7 constant_dynamic-update-slice_fusion.1
  29.4 0.7 constant_dynamic-update-slice_fusion
  30.1 15.4 %all-to-all-start = ((bf16[4,1,512,512]{3,0,1,2:T(4,128)(2,1)}), bf16[4,1,512,512]{3,0,1,2:T(4,128)(2,1)S(1)}, u32[]{:S(2)}, u32[]{:S(2)}) async-start(bf16[4,1,512,512]{3,0,1,2:T(4,128)(2,1)} %constant_dynamic-update-slice_fusion), calls=%async_computation | async-start | bytes 4194304 | tf_op jit(solution)/shard_map/all_to_all | solution.py:10
  45.6 100.1 %all-to-all-done = bf16[4,1,512,512]{3,0,1,2:T(4,128)(2,1)S(1)} async-done(((bf16[4,1,512,512]{3,0,1,2:T(4,128)(2,1)}), bf16[4,1,512,512]{3,0,1,2:T(4,128)(2,1)S(1)}, u32[]{:S(2)}, u32[]{:S(2)}) %all-to-all-start) | async-done | bytes 2097184 | tf_op jit(solution)/shard_map/all_to_all | solution.py:10
  145.6 0.4 copy.38
  146.0 1.0 select_bitcast_fusion
  147.1 1.8 copy.39
  148.9 108.6 %all-reduce.2.cloned.1.call-done = bf16[2,512,512]{2,1,0:T(8,128)(2,1)} async-done(((bf16[2,512,512]{2,1,0:T(8,128)(2,1)}), bf16[2,512,512]{2,1,0:T(8,128)(2,1)}) %all-reduce.2.cloned.1.call-update) | async-done | bytes 1048592 | tf_op jit(solution)/shard_map/psum | solution.py:16
  257.5 18.1 %while.13 = (s32[]{:T(128)}, bf16[2,512,512]{2,1,0:T(8,128)(2,1)S(1)}, s32[]{:T(128)}, s32[2]{0:T(128)S(1)}, bf16[4,512,512]{2,1,0:T(8,128)(2,1)}, /*index=5*/s3...) while((s32[]{:T(128)}, ...), condition=%wide.region_2.3_spmd, body=%wide.region_1.2_spmd.sunk | while | flops 268959776 | bytes 1573443 | solution.py:52
  258.2 0.6 dynamic_slice.51
  261.4 0.6 dynamic_slice.50
  264.6 1.7 fusion.15
  266.9 0.6 dynamic_slice.51
  270.1 0.6 dynamic_slice.50
  273.3 1.7 fusion.15
  275.7 1.0 copy-done.1
  (9 shorter events, 0.1 us)
Async XLA Ops:
  6.5 1.0 copy-start
  30.1 115.5 %all-to-all-start = ((bf16[4,1,512,512]{3,0,1,2:T(4,128)(2,1)}), bf16[4,1,512,512]{3,0,1,2:T(4,128)(2,1)S(1)}, u32[]{:S(2)}, u32[]{:S(2)}) async-start(bf16[4,1,512,512]{3,0,1,2:T(4,128)(2,1)} %constant_dynamic-update-slice_fusion), calls=%async_computation | async-start | bytes 4194304 | tf_op jit(solution)/shard_map/all_to_all | solution.py:10
  45.5 212.0 %all-reduce.2.cloned.1.call-start = ((), (), s32[]{:S(2)}) async-start(), calls=%async_computation.1 | async-start | bytes 2097152 | tf_op jit(solution)/shard_map/psum | solution.py:16
  147.1 110.4 %copy-start.2 = (s32[1,1,2]{2,1,0:T(1,128)S(1)}, s32[1,1,2]{2,1,0:T(1,128)}, u32[]{:S(2)}) copy-start(s32[1,1,2]{2,1,0:T(1,128)} %param.9) | copy-start | bytes 28
  147.1 110.4 %copy-start.3 = (s32[1,1,2]{2,1,0:T(1,128)S(1)}, s32[1,1,2]{2,1,0:T(1,128)}, u32[]{:S(2)}) copy-start(s32[1,1,2]{2,1,0:T(1,128)} %param.10) | copy-start | bytes 28
  275.7 1.0 copy-start.1
Sparse Core Ops, SparseCore 0:
  147.2 110.1 all-reduce.1
